TPU v7x, 512 devices: a whole 4x4x16 slice. The times are simulated.
512 devices in a mesh: dp: 64 (over z_hi, y, x, core), tensor: 8 (over z_lo).
Axes of the slice: x: 4, y: 4, z: 16 (z_hi: 2, z_lo: 8; z = z_hi * 8 + z_lo), core: 2. Of those that a mesh axis runs over, the one named last changes fastest.
Arguments:
- hidden: bfloat16 [8192, 7168], P('dp'), may hold values from -6 to 6
- norm_gain: bfloat16 [7168], replicated, may hold values from 0.099609375 to 1.8984375
- learner_probe_proj: float32 [7168, 4096], P(('dp', 'tensor')), may hold values from -1 to 1
- learner_lookup_proj: float32 [7168, 1024], P(('dp', 'tensor')), may hold values from -3 to 3
- learner_content_proj: float32 [7168, 1024], P(('dp', 'tensor')), may hold values from -0.0625 to 0.0625
- lengths: int32 [4], replicated, may hold values from 1 to 4096, 8192 in all
Outputs:
- serving_combined: bfloat16 [7168, 6144], P('dp', 'tensor')
- spun_lookup_vectors: bfloat16 [8192, 1024], P('dp', 'tensor')
- content_vectors: bfloat16 [8192, 1024], P('dp', 'tensor')
- attention_mix: bfloat16 [8192, 4096], P('dp', 'tensor')
Inputs may be any that keep to these rules, and one draw needn't show every extreme that they name: `lengths`: 4 prompts that fill all 8192 tokens; the longest has exactly 4096 tokens.
All inputs are finite; a program needn't handle non-finite values.
Results may differ from a plain program's by a relative error of at most 0.006.
The roundings to bfloat16 on the way count: a program that leaves them out, or rounds other values in their place, can miss the bound.
Values may be sent and summed in bfloat16 or wider, within the bound.
A program may use at most 64 MiB of HBM per device.

v0:
```python
import math

import jax
import jax.numpy as jnp
from jax import lax
from jax.sharding import PartitionSpec as P

SHARED_KV_NUM = 8
QUARTET_SHARE = 4
PER_ATTN_DIM = 128


rope_theta = 5000000.0
norm_eps = 1e-05
masked_score = -1e30


def document_start(lengths, positions):
    ends = jnp.cumsum(lengths)
    starts = ends - lengths
    inside = (positions[:, None] >= starts[None, :]) & (positions[:, None] < ends[None, :])
    return jnp.sum(jnp.where(inside, starts[None, :], 0), axis=1)


def spin_pairs(content_entries, shift_amounts):
    half_dim = content_entries.shape[-1] // 2
    inverse = rope_theta ** (
        -2.0 * jnp.arange(half_dim, dtype=jnp.float32) / content_entries.shape[-1]
    )
    angles = shift_amounts.astype(jnp.float32)[:, None] * inverse[None, :]
    cosine = jnp.cos(angles)[:, None, :]
    sine = jnp.sin(angles)[:, None, :]
    first = content_entries[..., :half_dim]
    second = content_entries[..., half_dim:]
    return jnp.concatenate(
        [first * cosine - second * sine, second * cosine + first * sine], axis=-1
    )


def per_device(
    hidden, norm_gain, learner_probe_proj, learner_lookup_proj, learner_content_proj, lengths
):
    tok_rows = hidden.shape[0]
    learner_lines = learner_probe_proj.shape[0]
    combined_slab = jnp.concatenate(
        [
            learner_probe_proj.reshape(learner_lines, SHARED_KV_NUM, QUARTET_SHARE * PER_ATTN_DIM),
            learner_lookup_proj.reshape(learner_lines, SHARED_KV_NUM, PER_ATTN_DIM),
            learner_content_proj.reshape(learner_lines, SHARED_KV_NUM, PER_ATTN_DIM),
        ],
        axis=2,
    )
    combined_slab = combined_slab.reshape(
        learner_lines, SHARED_KV_NUM * (QUARTET_SHARE + 2) * PER_ATTN_DIM
    ).astype(jnp.bfloat16)
    serving_combined = lax.all_to_all(
        combined_slab, "tensor", split_axis=1, concat_axis=0, tiled=True
    )
    local_groups = serving_combined.shape[1] // ((QUARTET_SHARE + 2) * PER_ATTN_DIM)
    widened = hidden.astype(jnp.float32)
    scale = lax.rsqrt(jnp.mean(widened * widened, axis=1, keepdims=True) + norm_eps)
    normed = (widened * scale * norm_gain.astype(jnp.float32)[None, :]).astype(jnp.bfloat16)
    mapped_result = jnp.dot(
        normed,
        lax.all_gather(serving_combined, "dp", axis=0, tiled=True),
        preferred_element_type=jnp.float32,
    )
    mapped_result = mapped_result.reshape(tok_rows, local_groups, QUARTET_SHARE + 2, PER_ATTN_DIM)
    query_part = mapped_result[:, :, :QUARTET_SHARE, :]
    key_part = mapped_result[:, :, QUARTET_SHARE, :]
    value_part = mapped_result[:, :, QUARTET_SHARE + 1, :]
    my_index = lax.axis_index("dp") * tok_rows + jnp.arange(tok_rows, dtype=jnp.int32)
    my_start = document_start(lengths, my_index)
    shift_amounts = my_index - my_start
    query_rot = spin_pairs(
        query_part.reshape(tok_rows, local_groups * QUARTET_SHARE, PER_ATTN_DIM), shift_amounts
    ).astype(jnp.bfloat16)
    spun_lookup_vectors = (
        spin_pairs(key_part, shift_amounts)
        .astype(jnp.bfloat16)
        .reshape(tok_rows, local_groups * PER_ATTN_DIM)
    )
    content_vectors = value_part.astype(jnp.bfloat16).reshape(tok_rows, local_groups * PER_ATTN_DIM)
    probe_vectors = query_rot.reshape(
        tok_rows, local_groups, QUARTET_SHARE, PER_ATTN_DIM
    ).transpose(1, 2, 0, 3)
    inv_root = 1.0 / math.sqrt(PER_ATTN_DIM)
    initial = (
        jnp.full((local_groups, QUARTET_SHARE, tok_rows, 1), masked_score, jnp.float32),
        jnp.zeros((local_groups, QUARTET_SHARE, tok_rows, 1), jnp.float32),
        jnp.zeros((local_groups, QUARTET_SHARE, tok_rows, PER_ATTN_DIM), jnp.float32),
    )
    key_piece = lax.all_gather(spun_lookup_vectors, "dp", axis=0, tiled=True)
    value_piece = lax.all_gather(content_vectors, "dp", axis=0, tiled=True)
    span = key_piece.shape[0]
    step_size = math.gcd(span, 512)

    def one_step(turn, state):
        top, total, accum = state
        begin = turn * step_size
        keys_three = lax.dynamic_slice_in_dim(key_piece, begin, step_size, 0).reshape(
            step_size, local_groups, PER_ATTN_DIM
        )
        values_three = lax.dynamic_slice_in_dim(value_piece, begin, step_size, 0).reshape(
            step_size, local_groups, PER_ATTN_DIM
        )
        key_index = begin + jnp.arange(step_size, dtype=jnp.int32)
        key_start = document_start(lengths, key_index)
        allowed = (
            (key_start[None, :] == my_start[:, None])
            & (key_index[None, :] <= my_index[:, None])
            & (key_index[None, :] >= 0)
        )
        scores = (
            jnp.einsum(
                "ghqd,kgd->ghqk", probe_vectors, keys_three, preferred_element_type=jnp.float32
            )
            * inv_root
        )
        scores = jnp.where(allowed, scores, masked_score)
        new_top = jnp.maximum(top, jnp.max(scores, axis=3, keepdims=True))
        weights = jnp.where(allowed, jnp.exp(scores - new_top), 0.0)
        fade = jnp.exp(top - new_top)
        total = total * fade + jnp.sum(weights, axis=3, keepdims=True)
        accum = accum * fade + jnp.einsum(
            "ghqk,kgd->ghqd",
            weights.astype(jnp.bfloat16),
            values_three,
            preferred_element_type=jnp.float32,
        )
        return (new_top, total, accum)

    top, total, accum = lax.fori_loop(0, span // step_size, one_step, initial)
    attention_mix = (
        (accum / total)
        .transpose(2, 0, 1, 3)
        .reshape(tok_rows, local_groups * QUARTET_SHARE * PER_ATTN_DIM)
        .astype(jnp.bfloat16)
    )
    return (serving_combined, spun_lookup_vectors, content_vectors, attention_mix)


def solution(mesh):
    in_specs = (
        P("dp", None),
        P(),
        P(("dp", "tensor"), None),
        P(("dp", "tensor"), None),
        P(("dp", "tensor"), None),
        P(),
    )
    out_specs = (P("dp", "tensor"), P("dp", "tensor"), P("dp", "tensor"), P("dp", "tensor"))
    return jax.shard_map(
        per_device, mesh=mesh, in_specs=in_specs, out_specs=out_specs, check_vma=False
    )
```

profile of v0, /device:TPU:25, one launch (start us, length us, event | category | flops | bytes accessed | tf_op | source)
XLA Modules:
  0.0 519.0 jit_solution(11853927913297743682)
XLA Ops:
  7.2 1.0 convert.33
  8.3 0.8 convert.32
  9.1 1.0 convert.31
  10.2 23.2 %all_to_all.16 = bf16[14,8,768]{2,0,1:T(8,128)(2,1)S(1)} all-to-all(bf16[14,8,768]{2,0,1:T(8,128)(2,1)S(1)} %pad_maximum_fusion), channel_id=1, replica_groups=mesh['dp'=64,'tensor'=8] {'tensor'}, dimensions={1} | all-to-all | bytes 344064 | tf_op jit(solution)/shard_map/all_to_all | solution.py:56
  33.4 0.7 all_to_all.14
  34.6 0.4 fusion.20
  35.0 194.1 %all-gather.5.cloned.1.call-done = bf16[7168,768]{1,0:T(8,128)(2,1)} async-done(((bf16[112,768]{1,0:T(8,128)(2,1)}), bf16[7168,768]{1,0:T(8,128)(2,1)}) %all-gather.5.cloned.1.call-update) | async-done | bytes 11010064 | tf_op jit(solution)/shard_map/all_gather | solution.py:65
  229.1 7.2 %fusion.23 = f32[128,768]{0,1:T(8,128)S(1)} fusion(bf16[7168,768]{1,0:T(8,128)(2,1)} %all-gather.5.cloned.1.call-done, bf16[128,7168]{1,0:T(8,128)(2,1)S(1)} %copy-done, f32[7168]{0:T(1024)S(1)} %convert_element_type.58, f32[128]{0:T(128)S(1)} %add_rsqrt_fusion), kind=kOutput, calls=%fused_computation.36 | convolution fusion | flops 1412956160 | bytes 13267456 | tf_op jit(solution)/shard_map/dot_general | solution.py:63
  236.5 0.6 pad_maximum_fusion.1
  237.2 0.6 slice.66
  238.1 1.5 copy.38
  239.6 0.7 copy.39
  240.6 106.6 %all-gather.7.cloned.1.call-done = bf16[8192,128]{0,1:T(8,128)(2,1)} async-done(((bf16[128,128]{0,1:T(8,128)(2,1)}), bf16[8192,128]{0,1:T(8,128)(2,1)}) %all-gather.7.cloned.1.call-update) | async-done | bytes 2097168 | tf_op jit(solution)/shard_map/all_gather | solution.py:93
  347.1 112.0 %all-gather.9.cloned.1.call-done = bf16[8192,1,1,128]{0,3,2,1:T(8,128)(2,1)} async-done(((bf16[128,1,1,128]{0,3,2,1:T(8,128)(2,1)}), bf16[8192,1,1,128]{0,3,2,1:T(8,128)(2,1)}) %all-gather.9.cloned.1.call-update) | async-done | bytes 2097168 | tf_op jit(solution)/shard_map/all_gather | solution.py:94
  459.1 52.4 %while.20 = (s32[]{:T(128)}, f32[1,4,128,1]{2,1,3,0:T(4,128)S(1)}, f32[1,4,128,1]{2,1,3,0:T(4,128)S(1)}, f32[1,4,128,128]{3,2,1,0:T(8,128)S(1)}, s32[1,4]{1,0:T(...) while((s32[]{:T(128)}, f32[1,4,128,1]{2,1,3,0:T(4,128)S(1)}, ...), condition=%wide.region_7.8_spmd.clone, body=%wide.region_3.7_spmd.clone.sunk | while | flops 137050240 | bytes 4371203 | solution.py:133
  459.3 0.3 and_and_fusion.2
  459.5 1.2 fusion.50
  461.0 1.3 fusion.53
  462.5 0.3 and_and_fusion.2
  462.8 1.2 fusion.50
  464.3 1.3 fusion.53
  465.8 0.3 and_and_fusion.2
  466.1 1.2 fusion.50
  467.6 1.3 fusion.53
  469.1 0.3 and_and_fusion.2
  469.4 1.2 fusion.50
  470.9 1.3 fusion.53
  472.4 0.3 and_and_fusion.2
  472.6 1.2 fusion.50
  474.1 1.3 fusion.53
  475.6 0.3 and_and_fusion.2
  475.9 1.2 fusion.50
  477.4 1.3 fusion.53
  478.9 0.3 and_and_fusion.2
  479.2 1.2 fusion.50
  480.7 1.3 fusion.53
  482.2 0.3 and_and_fusion.2
  482.5 1.2 fusion.50
  484.0 1.3 fusion.53
  485.5 0.3 and_and_fusion.2
  485.7 1.2 fusion.50
  487.3 1.3 fusion.53
  488.8 0.3 and_and_fusion.2
  489.0 1.2 fusion.50
  490.5 1.3 fusion.53
  492.0 0.3 and_and_fusion.2
  492.3 1.2 fusion.50
  493.8 1.3 fusion.53
  495.3 0.3 and_and_fusion.2
  495.6 1.2 fusion.50
  497.1 1.3 fusion.53
  498.6 0.3 and_and_fusion.2
  498.9 1.2 fusion.50
  500.4 1.3 fusion.53
  501.9 0.3 and_and_fusion.2
  502.1 1.2 fusion.50
  503.6 1.3 fusion.53
  505.1 0.3 and_and_fusion.2
  505.4 1.2 fusion.50
  506.9 1.3 fusion.53
  508.4 0.3 and_and_fusion.2
  508.7 1.2 fusion.50
  510.2 1.3 fusion.53
  511.8 0.7 copy.49
  (171 shorter events, 6.9 us)
Async XLA Ops:
  7.2 27.1 %copy-start.1 = (bf16[7168]{0:T(1024)(128)(2,1)S(1)}, bf16[7168]{0:T(1024)(128)(2,1)}, u32[]{:S(2)}) copy-start(bf16[7168]{0:T(1024)(128)(2,1)} %param.9) | copy-start | bytes 43012
  7.2 27.1 %copy-start.2 = (s32[4]{0:T(128)S(1)}, s32[4]{0:T(128)}, u32[]{:S(2)}) copy-start(s32[4]{0:T(128)} %param.13) | copy-start | bytes 52
  7.2 27.4 %copy-start = (bf16[128,7168]{1,0:T(8,128)(2,1)S(1)}, bf16[128,7168]{1,0:T(8,128)(2,1)}, u32[]{:S(2)}) copy-start(bf16[128,7168]{1,0:T(8,128)(2,1)} %param.8) | copy-start | bytes 5505028
  7.2 221.9 %all-gather.5.cloned.1.call-start = ((), (), s32[]{:S(2)}) async-start(), calls=%async_computation.1 | async-start | bytes 11182080 | tf_op jit(solution)/shard_map/all_gather | solution.py:65
  34.2 312.9 %all-gather.7.cloned.1.call-start = ((), (), s32[]{:S(2)}) async-start(), calls=%async_computation.2 | async-start | bytes 2129920 | tf_op jit(solution)/shard_map/all_gather | solution.py:93
  237.2 222.0 %all-gather.9.cloned.1.call-start = ((), (), s32[]{:S(2)}) async-start(), calls=%async_computation.3 | async-start | bytes 2129920 | tf_op jit(solution)/shard_map/all_gather | solution.py:94
Sparse Core Ops, SparseCore 0:
  34.3 194.7 all-gather.4
  237.3 109.7 all-gather.6
  351.3 107.7 all-gather.8
where the time goes:
time: 521 us; the launch traced here: 519 us
  waiting for transfers between devices  413 us (79%)
  matrix products  48.6 us (9%)
  blocking collectives  23.2 us (4%)
  other arithmetic  14.5 us (3%)
  between operations  14 us (3%)
    all_gather x1, waiting for transfers between devices, per_device(): lax.all_gather(serving_combined, 'dp', axis=0, tiled=True)  194 us
    all_gather x1, waiting for transfers between devices, per_device(): value_piece = lax.all_gather(content_vectors, 'dp', axis=0, tiled=True)  112 us
    all_gather x1, waiting for transfers between devices, per_device(): key_piece = lax.all_gather(spun_lookup_vectors, 'dp', axis=0, tiled=True)  107 us
    all_to_all x1, blocking collectives, per_device(): lax.all_to_all(combined_slab, 'tensor', split_axis=1, concat_axis=0, tile...  23.2 us
    dot_general x16, matrix products, one_step(): jnp.einsum('ghqk,kgd->ghqd', weights.astype(jnp.bfloat16), values_three,...  21.5 us
    dot_general x16, matrix products, one_step(): jnp.einsum('ghqd,kgd->ghqk', probe_vectors, keys_three, preferred_element...  19.9 us
  transfers between devices with their start and end apart: 3, of which 3 were waited for; matrix products, arithmetic and copies ran while one was open for 1% of the time, Pallas kernels for 0%

commit v1 on v0

v1 whole, which is shorter than its diff:
```python
import functools
import math

import jax
import jax.numpy as jnp
from jax import lax
from jax.experimental import pallas as pl
from jax.experimental.pallas import tpu as pltpu
from jax.sharding import PartitionSpec as P

SHARED_KV_NUM = 8
QUARTET_SHARE = 4
PER_ATTN_DIM = 128
MAXLEN = 4096

rope_theta = 5000000.0
norm_eps = 1e-05
masked_score = -1e30

RING = 4


def document_start(lengths, positions):
    ends = jnp.cumsum(lengths)
    starts = ends - lengths
    inside = (positions[:, None] >= starts[None, :]) & (positions[:, None] < ends[None, :])
    return jnp.sum(jnp.where(inside, starts[None, :], 0), axis=1)


def spread(source, slot, send_sem, recv_sem):
    me = lax.axis_index("dp")
    core = me % 2
    x = (me // 2) % RING
    y = (me // (2 * RING)) % RING
    z = me // (2 * RING * RING)

    def index(dz, dy, dx, other=False):
        c = 1 - core if other else core
        return ((((z + dz) % 2) * RING + (y + dy + RING) % RING) * RING + (x + dx + RING) % RING) * 2 + c

    def along(half, dz, first, second):
        return index(dz, second, first) if half == 0 else index(dz, first, second)

    sibling = index(0, 0, 0, True)
    antipode = index(1, 0, 0)
    barrier = pltpu.get_barrier_semaphore()
    partners = [index(0, 0, 1), index(0, 0, -1), index(0, 1, 0), index(0, -1, 0), antipode, sibling]
    for partner in partners:
        pl.semaphore_signal(
            barrier, inc=1, device_id={"dp": partner}, device_id_type=pl.DeviceIdType.MESH
        )
    pl.semaphore_wait(barrier, len(partners))

    sent = []

    def push(src, origin, half, target):
        copy = pltpu.make_async_remote_copy(
            src_ref=src,
            dst_ref=slot(origin, half),
            send_sem=send_sem.at[len(sent)],
            recv_sem=recv_sem.at[origin, half],
            device_id={"dp": target},
            device_id_type=pl.DeviceIdType.MESH,
        )
        copy.start()
        sent.append(copy)

    def landed(origin, half):
        there = slot(origin, half)
        pltpu.make_async_copy(there, there, recv_sem.at[origin, half]).wait()

    def forward(src, half, dz, first, second):
        origin = along(half, dz, first, second)
        if second == 0:
            if first == 0:
                push(src, origin, half, along(half, 0, 1, 0))
                push(src, origin, half, along(half, 0, -1, 0))
            if first == -1 and dz == 0:
                push(src, origin, half, along(half, 0, 1, 0))
            if first == 1 and dz == 1:
                push(src, origin, half, along(half, 0, -1, 0))
            push(src, origin, half, along(half, 0, 0, 1))
            push(src, origin, half, along(half, 0, 0, -1))
        upward = (abs(first) + dz) % 2 == 0
        if second == -1 and upward:
            push(src, origin, half, along(half, 0, 0, 1))
        if second == 1 and not upward:
            push(src, origin, half, along(half, 0, 0, -1))
        push(src, origin, half, sibling)

    offsets = [(f, s) for f in (0, -1, 1, 2) for s in (0, -1, 1, 2)]
    offsets.sort(key=lambda pair: abs(pair[0]) + abs(pair[1]))
    for half in range(2):
        push(source(half), me, half, antipode)
    for half in range(2):
        forward(source(half), half, 0, 0, 0)
    for dz in range(2):
        for first, second in offsets:
            if (dz, first, second) == (0, 0, 0):
                continue
            for half in range(2):
                origin = along(half, dz, first, second)
                landed(origin, half)
                forward(slot(origin, half), half, dz, first, second)
    for dz in range(2):
        for first, second in offsets:
            for half in range(2):
                origin = along(half, dz, first, second) + 1 - 2 * core
                landed(origin, half)
    for copy in sent:
        copy.wait_send()


SENDS = 2 * (1 + 2 * (3 + 12 + 16))


def project_kernel(normed_ref, block_ref, cos_ref, sin_ref, q_ref, kv_ref, buf, send_sem, recv_sem):
    rows, width = block_ref.shape
    part = width // 2
    me = lax.axis_index("dp")

    def slot(origin, half):
        return buf.at[half, pl.ds(pl.multiple_of(origin * rows, rows), rows), :]

    def source(half):
        return block_ref.at[:, pl.ds(half * part, part)]

    own = pl.ds(pl.multiple_of(me * rows, rows), rows)
    for half in range(2):
        buf[half, own, :] = block_ref[:, half * part : (half + 1) * part]
    spread(source, slot, send_sem, recv_sem)
    cosine = cos_ref[...]
    sine = sin_ref[...]
    heads = part // PER_ATTN_DIM
    for half in range(2):
        mapped = jnp.dot(normed_ref[...], buf[half], preferred_element_type=jnp.float32)
        for j in range(heads):
            head = half * heads + j
            vec = mapped[:, j * PER_ATTN_DIM : (j + 1) * PER_ATTN_DIM]
            if head <= QUARTET_SHARE:
                vec = vec * cosine + pltpu.roll(vec, PER_ATTN_DIM // 2, 1) * sine
            if head < QUARTET_SHARE:
                q_ref[head] = vec.astype(jnp.bfloat16)
            else:
                kv_ref[head - QUARTET_SHARE] = vec.astype(jnp.bfloat16)


def attend_kernel(q_ref, kv_ref, start_ref, mix_ref, buf, send_sem, recv_sem):
    _, rows, width = kv_ref.shape
    me = lax.axis_index("dp")

    def slot(origin, half):
        return buf.at[half, pl.ds(pl.multiple_of(origin * rows, rows), rows), :]

    def source(half):
        return kv_ref.at[half]

    own = pl.ds(pl.multiple_of(me * rows, rows), rows)
    for half in range(2):
        buf[half, own, :] = kv_ref[half]
    spread(source, slot, send_sem, recv_sem)

    lines = QUARTET_SHARE * rows
    step = 512
    inv_root = 1.0 / math.sqrt(PER_ATTN_DIM)
    queries = q_ref[...].reshape(lines, width)
    q_start = start_ref[...]
    q_index = me * rows + lax.broadcasted_iota(jnp.int32, (lines, 1), 0) % rows
    back = MAXLEN // rows
    low = (jnp.maximum(me - back, 0) * rows) // step
    high = ((me + 1) * rows + step - 1) // step

    def one_step(turn, state):
        top, total, accum = state
        begin = pl.multiple_of(turn * step, step)
        keys = buf[0, pl.ds(begin, step), :]
        values = buf[1, pl.ds(begin, step), :]
        key_index = begin + lax.broadcasted_iota(jnp.int32, (1, step), 1)
        allowed = (key_index <= q_index) & (key_index >= q_start)
        scores = (
            lax.dot_general(
                queries, keys, (((1,), (1,)), ((), ())), preferred_element_type=jnp.float32
            )
            * inv_root
        )
        scores = jnp.where(allowed, scores, masked_score)
        new_top = jnp.maximum(top, jnp.max(scores, axis=1, keepdims=True))
        weights = jnp.where(allowed, jnp.exp(scores - new_top), 0.0)
        fade = jnp.exp(top - new_top)
        total = total * fade + jnp.sum(weights, axis=1, keepdims=True)
        accum = accum * fade + jnp.dot(
            weights.astype(jnp.bfloat16), values, preferred_element_type=jnp.float32
        )
        return new_top, total, accum

    initial = (
        jnp.full((lines, 1), masked_score, jnp.float32),
        jnp.zeros((lines, 1), jnp.float32),
        jnp.zeros((lines, width), jnp.float32),
    )
    top, total, accum = lax.fori_loop(low, high, one_step, initial)
    mix = (accum / total).astype(jnp.bfloat16)
    for j in range(QUARTET_SHARE):
        mix_ref[:, j * width : (j + 1) * width] = mix[j * rows : (j + 1) * rows]


def per_device(
    hidden, norm_gain, learner_probe_proj, learner_lookup_proj, learner_content_proj, lengths
):
    tok_rows = hidden.shape[0]
    learner_lines = learner_probe_proj.shape[0]
    group_width = (QUARTET_SHARE + 2) * PER_ATTN_DIM
    combined_slab = jnp.concatenate(
        [
            learner_probe_proj.reshape(learner_lines, SHARED_KV_NUM, QUARTET_SHARE * PER_ATTN_DIM),
            learner_lookup_proj.reshape(learner_lines, SHARED_KV_NUM, PER_ATTN_DIM),
            learner_content_proj.reshape(learner_lines, SHARED_KV_NUM, PER_ATTN_DIM),
        ],
        axis=2,
    )
    combined_slab = combined_slab.reshape(learner_lines, SHARED_KV_NUM * group_width).astype(
        jnp.bfloat16
    )
    serving_combined = lax.all_to_all(
        combined_slab, "tensor", split_axis=1, concat_axis=0, tiled=True
    )
    widened = hidden.astype(jnp.float32)
    scale = lax.rsqrt(jnp.mean(widened * widened, axis=1, keepdims=True) + norm_eps)
    normed = (widened * scale * norm_gain.astype(jnp.float32)[None, :]).astype(jnp.bfloat16)

    my_index = lax.axis_index("dp") * tok_rows + jnp.arange(tok_rows, dtype=jnp.int32)
    my_start = document_start(lengths, my_index)
    half_dim = PER_ATTN_DIM // 2
    inverse = rope_theta ** (-2.0 * jnp.arange(half_dim, dtype=jnp.float32) / PER_ATTN_DIM)
    angles = (my_index - my_start).astype(jnp.float32)[:, None] * inverse[None, :]
    cosine = jnp.cos(angles)
    sine = jnp.sin(angles)
    cosine = jnp.concatenate([cosine, cosine], axis=1)
    sine = jnp.concatenate([-sine, sine], axis=1)

    rows = serving_combined.shape[0]
    devices = 64
    vmem = pl.BlockSpec(memory_space=pltpu.VMEM)
    semaphores = [pltpu.SemaphoreType.DMA((SENDS,)), pltpu.SemaphoreType.DMA((devices, 2))]
    queries, keys_values = pl.pallas_call(
        project_kernel,
        out_shape=(
            jax.ShapeDtypeStruct((QUARTET_SHARE, tok_rows, PER_ATTN_DIM), jnp.bfloat16),
            jax.ShapeDtypeStruct((2, tok_rows, PER_ATTN_DIM), jnp.bfloat16),
        ),
        in_specs=[vmem] * 4,
        out_specs=(vmem, vmem),
        scratch_shapes=[pltpu.VMEM((2, rows * devices, group_width // 2), jnp.bfloat16)]
        + semaphores,
        compiler_params=pltpu.CompilerParams(
            collective_id=0, has_side_effects=True, vmem_limit_bytes=48 * 2**20
        ),
        name="project",
    )(normed, serving_combined, cosine, sine)
    starts = jnp.tile(my_start, QUARTET_SHARE)[:, None]
    attention_mix = pl.pallas_call(
        attend_kernel,
        out_shape=jax.ShapeDtypeStruct((tok_rows, QUARTET_SHARE * PER_ATTN_DIM), jnp.bfloat16),
        in_specs=[vmem] * 3,
        out_specs=vmem,
        scratch_shapes=[pltpu.VMEM((2, tok_rows * devices, PER_ATTN_DIM), jnp.bfloat16)]
        + semaphores,
        compiler_params=pltpu.CompilerParams(
            collective_id=1, has_side_effects=True, vmem_limit_bytes=48 * 2**20
        ),
        name="attend",
    )(queries, keys_values, starts)
    return (serving_combined, keys_values[0], keys_values[1], attention_mix)


def solution(mesh):
    in_specs = (
        P("dp", None),
        P(),
        P(("dp", "tensor"), None),
        P(("dp", "tensor"), None),
        P(("dp", "tensor"), None),
        P(),
    )
    out_specs = (P("dp", "tensor"), P("dp", "tensor"), P("dp", "tensor"), P("dp", "tensor"))
    return jax.shard_map(
        per_device, mesh=mesh, in_specs=in_specs, out_specs=out_specs, check_vma=False
    )
```

time: 521 us -> 139 us (0.27)
  waiting for transfers between devices: 413 us -> 8.22 us
  Pallas kernels: 0 us -> 108 us
  matrix products: 48.6 us -> 0 us
  blocking collectives: 23.2 us -> 0 us
  between operations: 14 us -> 0.81 us
  starting transfers between devices: 0.12 us -> 12.2 us
  other arithmetic: 14.5 us -> 5.15 us
    all_gather x3 -> x0, waiting for transfers between devices: 413 us -> none  [the longest x1 194 us: per_device(): lax.all_gather(serving_combined, 'dp', axis=0, tiled=True)]
    pallas_call x0 -> x2, Pallas kernels: none -> 108 us  [the longest x1 61.2 us: per_device(): pl.pallas_call(project_kernel, out_shape=(jax.ShapeDtypeStruct((QUARTET_S...]
    dot_general x33 -> x0, matrix products: 48.6 us -> none  [the longest x16 21.5 us: one_step(): jnp.einsum('ghqk,kgd->ghqd', weights.astype(jnp.bfloat16), values_three,...]
    all_to_all x1 -> x0, blocking collectives: 23.2 us -> none  [per_device(): lax.all_to_all(combined_slab, 'tensor', split_axis=1, concat_axis=0, tile...]
    all_to_all x0 -> x1, starting transfers between devices: none -> 12.2 us  [per_device(): lax.all_to_all(combined_slab, 'tensor', split_axis=1, concat_axis=0, tile...]
    all_to_all x0 -> x1, waiting for transfers between devices: none -> 8.22 us  [per_device(): lax.all_to_all(combined_slab, 'tensor', split_axis=1, concat_axis=0, tile...]
  transfers between devices with their start and end apart: 3 -> 1, of which waited for: 3 -> 1; matrix products, arithmetic and copies ran while one was open for 1% -> 1% of each run, Pallas kernels for 0% -> 0%
where the time goes in v1:
time: 139 us; the launch traced here: 137 us
  Pallas kernels  108 us (78%)
  starting transfers between devices  12.2 us (9%)
  waiting for transfers between devices  8.22 us (6%)
  other arithmetic  5.15 us (4%)
  local copies, waits for them, and re-layouts  2.68 us (2%)
    pallas_call x1, Pallas kernels, per_device(): pl.pallas_call(project_kernel, out_shape=(jax.ShapeDtypeStruct((QUARTET_S...  61.2 us
    pallas_call x1, Pallas kernels, per_device(): pl.pallas_call(attend_kernel, out_shape=jax.ShapeDtypeStruct((tok_rows, Q...  47.2 us
    all_to_all x1, starting transfers between devices, per_device(): lax.all_to_all(combined_slab, 'tensor', split_axis=1, concat_axis=0, tile...  12.2 us
    all_to_all x1, waiting for transfers between devices, per_device(): lax.all_to_all(combined_slab, 'tensor', split_axis=1, concat_axis=0, tile...  8.22 us
    another operation x4, other arithmetic  2.97 us
  transfers between devices with their start and end apart: 1, of which 1 were waited for; matrix products, arithmetic and copies ran while one was open for 1% of the time, Pallas kernels for 0%

profile of v1, /device:TPU:25, one launch (start us, length us, event | category | flops | bytes accessed | tf_op | source)
XLA Modules:
  0.0 137.5 jit_solution(484587878483472661)
XLA Ops:
  0.6 0.0 copy-start.4
  0.6 0.0 copy-start.3
  0.7 0.0 copy-start.1
  0.7 1.1 convert.12
  1.9 0.8 convert.13
  2.8 0.8 convert.14
  3.6 0.7 pad_maximum_fusion
  4.3 12.2 %all-to-all-start = ((bf16[14,8,768]{2,0,1:T(8,128)(2,1)}), bf16[14,8,768]{2,0,1:T(8,128)(2,1)S(1)}, u32[]{:S(2)}, u32[]{:S(2)}) async-start(bf16[14,8,768]{2,0,1:T(8,128)(2,1)} %pad_maximum_fusion), calls=%async_computation | async-start | bytes 393216 | tf_op jit(solution)/shard_map/all_to_all | solution.py:224
  16.6 0.0 copy-done.4
  16.6 0.2 reduce-window.8
  16.8 0.0 copy-start.2
  16.8 0.0 copy-done.3
  16.8 0.0 copy-done.1
  16.8 0.4 fusion
  17.3 1.0 copy-done.2
  18.3 0.5 fusion.2.normed_ref
  18.8 0.1 select_reduce_fusion
  18.9 0.2 copy.20.start_ref
  19.1 0.3 fusion.3
  19.4 0.1 pad_maximum_fusion.1
  19.5 8.2 %all-to-all-done = bf16[14,8,768]{2,0,1:T(8,128)(2,1)S(1)} async-done(((bf16[14,8,768]{2,0,1:T(8,128)(2,1)}), bf16[14,8,768]{2,0,1:T(8,128)(2,1)S(1)}, u32[]{:S(2)}, u32[]{:S(2)}) %all-to-all-start) | async-done | bytes 172064 | tf_op jit(solution)/shard_map/all_to_all | solution.py:224
  27.7 0.1 all_to_all.14.block_ref
  27.8 0.0 copy-start
  27.8 61.2 %project.1 = (bf16[4,128,128]{2,1,0:T(8,128)(2,1)S(1)}, bf16[2,128,128]{2,1,0:T(8,128)(2,1)S(1)}) custom-call(bf16[128,7168]{1,0:T(8,128)(2,1)S(1)} %fusion.2.normed_ref, bf16[112,768]{1,0:T(8,128)(2,1)S(1)} %all_to_all.14.block_ref, f32[128,128]{1,0:T(8,128)S(1)} %get-tuple-element.13.cos_ref, f32[128,128]{1,0:T(8,128)S(1)} %get-tuple-element.14.sin_ref), custom_call_target="tpu_custom_call" | custom-call | tf_op jit(solution)/shard_map/project/pallas_call | solution.py:245
  89.0 0.6 slice_bitcast_fusion
  89.6 47.2 %attend.1 = bf16[128,512]{1,0:T(8,128)(2,1)S(1)} custom-call(bf16[4,128,128]{2,1,0:T(8,128)(2,1)S(1)} %get-tuple-element.7.q_ref, bf16[2,128,128]{2,1,0:T(8,128)(2,1)S(1)} %get-tuple-element.6.kv_ref, s32[512,1]{1,0:T(8,128)S(1)} %copy.20.start_ref), custom_call_target="tpu_custom_call" | custom-call | tf_op jit(solution)/shard_map/attend/pallas_call | solution.py:261
  136.8 0.7 copy.25
  137.5 0.0 copy-done
  (16 shorter events, 0.2 us)
Async XLA Ops:
  0.6 16.0 %copy-start.4 = (s32[4]{0:T(128)S(1)}, s32[4]{0:T(128)}, u32[]{:S(2)}) copy-start(s32[4]{0:T(128)} %param.11) | copy-start | bytes 52
  0.6 16.1 %copy-start.3 = (bf16[7168]{0:T(1024)(128)(2,1)S(1)}, bf16[7168]{0:T(1024)(128)(2,1)}, u32[]{:S(2)}) copy-start(bf16[7168]{0:T(1024)(128)(2,1)} %param.7) | copy-start | bytes 43012
  0.7 16.1 %copy-start.1 = (bf16[128,7168]{1,0:T(8,128)(2,1)S(1)}, bf16[128,7168]{1,0:T(8,128)(2,1)}, u32[]{:S(2)}) copy-start(bf16[128,7168]{1,0:T(8,128)(2,1)} %param.6) | copy-start | bytes 5505028
  4.3 23.4 %all-to-all-start = ((bf16[14,8,768]{2,0,1:T(8,128)(2,1)}), bf16[14,8,768]{2,0,1:T(8,128)(2,1)S(1)}, u32[]{:S(2)}, u32[]{:S(2)}) async-start(bf16[14,8,768]{2,0,1:T(8,128)(2,1)} %pad_maximum_fusion), calls=%async_computation | async-start | bytes 393216 | tf_op jit(solution)/shard_map/all_to_all | solution.py:224
  16.8 1.5 %copy-start.2 = (bf16[128,7168]{1,0:T(8,128)(2,1)S(1)}, bf16[128,7168]{1,0:T(8,128)(2,1)}, u32[]{:S(2)}) copy-start(bf16[128,7168]{1,0:T(8,128)(2,1)} %param.6) | copy-start | bytes 5505028
  27.8 109.7 %copy-start = (bf16[112,768]{1,0:T(8,128)(2,1)}, bf16[112,768]{1,0:T(8,128)(2,1)S(1)}, u32[]{:S(2)}) copy-start(bf16[112,768]{1,0:T(8,128)(2,1)S(1)} %all_to_all.14.block_ref) | copy-start | bytes 516100

commit v2 on v1

v2 whole, which is shorter than its diff:
```python
import math

import jax
import jax.numpy as jnp
from jax import lax
from jax.experimental import pallas as pl
from jax.experimental.pallas import tpu as pltpu
from jax.sharding import PartitionSpec as P

SHARED_KV_NUM = 8
QUARTET_SHARE = 4
PER_ATTN_DIM = 128
MAXLEN = 4096

rope_theta = 5000000.0
norm_eps = 1e-05
masked_score = -1e30

RING = 4


def document_start(lengths, positions):
    ends = jnp.cumsum(lengths)
    starts = ends - lengths
    inside = (positions[:, None] >= starts[None, :]) & (positions[:, None] < ends[None, :])
    return jnp.sum(jnp.where(inside, starts[None, :], 0), axis=1)


def neighbour_index(dz=0, dy=0, dx=0, other=False):
    me = lax.axis_index("dp")
    core = 1 - me % 2 if other else me % 2
    x = (me // 2) % RING
    y = (me // (2 * RING)) % RING
    z = me // (2 * RING * RING)
    return ((((z + dz) % 2) * RING + (y + dy + RING) % RING) * RING + (x + dx + RING) % RING) * 2 + core


def z_chip(shift):
    plane = 2 * RING * RING
    me = lax.axis_index("dp")
    place = (me // plane) * SHARED_KV_NUM + lax.axis_index("tensor") + shift
    place = (place + 2 * SHARED_KV_NUM) % (2 * SHARED_KV_NUM)
    return (place // SHARED_KV_NUM) * plane + me % plane, place % SHARED_KV_NUM


def greet():
    barrier = pltpu.get_barrier_semaphore()
    tensor = lax.axis_index("tensor")
    partners = [
        (neighbour_index(0, 0, 1), tensor),
        (neighbour_index(0, 0, -1), tensor),
        (neighbour_index(0, 1, 0), tensor),
        (neighbour_index(0, -1, 0), tensor),
        (neighbour_index(0, 0, 0, True), tensor),
        z_chip(Z_STEP),
        z_chip(-Z_STEP),
    ]
    for partner in partners:
        pl.semaphore_signal(
            barrier, inc=1, device_id=partner, device_id_type=pl.DeviceIdType.MESH
        )
    pl.semaphore_wait(barrier, len(partners))


def spread(source, slot, relay, send_sem, recv_sem, relay_sem, started=None, middle=None):
    me = lax.axis_index("dp")
    core = me % 2
    tensor = lax.axis_index("tensor")
    index = neighbour_index

    def along(half, dz, first, second):
        return index(dz, second, first) if half == 0 else index(dz, first, second)

    sibling = index(0, 0, 0, True)
    sent = []

    def push(src, dst, target, arrival):
        copy = pltpu.make_async_remote_copy(
            src_ref=src,
            dst_ref=dst,
            send_sem=send_sem.at[len(sent)],
            recv_sem=arrival,
            device_id=target,
            device_id_type=pl.DeviceIdType.MESH,
        )
        copy.start()
        sent.append(copy)

    def landed(there, arrival):
        pltpu.make_async_copy(there, there, arrival).wait()

    def forward(src, half, dz, first, second):
        origin = along(half, dz, first, second)

        def give(dfirst, dsecond):
            target = (along(half, 0, dfirst, dsecond), tensor)
            push(src, slot(origin, half), target, recv_sem.at[origin, half])

        if second == 0:
            if first == 0:
                give(1, 0)
                give(-1, 0)
            if first == -1 and dz == 0:
                give(1, 0)
            if first == 1 and dz == 1:
                give(-1, 0)
            give(0, 1)
            give(0, -1)
        upward = (abs(first) + dz) % 2 == 0
        if second == -1 and upward:
            give(0, 1)
        if second == 1 and not upward:
            give(0, -1)
        push(src, slot(origin, half), (sibling, tensor), recv_sem.at[origin, half])

    offsets = [(f, s) for f in (0, -1, 1, 2) for s in (0, -1, 1, 2)]
    offsets.sort(key=lambda pair: abs(pair[0]) + abs(pair[1]))

    def receive(dz, hops):
        for first, second in offsets:
            if abs(first) + abs(second) == hops:
                for half in range(2):
                    origin = along(half, dz, first, second)
                    landed(slot(origin, half), recv_sem.at[origin, half])
                    forward(slot(origin, half), half, dz, first, second)

    def from_sibling(dz):
        for first, second in offsets:
            for half in range(2):
                origin = along(half, dz, first, second) + 1 - 2 * core
                landed(slot(origin, half), recv_sem.at[origin, half])

    for half in range(2):
        push(source(half), relay.at[half], z_chip(Z_STEP - 2 * Z_STEP * half), relay_sem.at[half])
    for half in range(2):
        forward(source(half), half, 0, 0, 0)
    if started is not None:
        started()
    receive(0, 1)
    for half in range(2):
        shift = Z_STEP - 2 * Z_STEP * half
        origin, _ = z_chip(-shift)
        landed(relay.at[half], relay_sem.at[half])
        push(relay.at[half], slot(origin, half), z_chip(shift), recv_sem.at[origin, half])
    for hops in range(2, 5):
        receive(0, hops)
    if middle is not None:
        from_sibling(0)
        middle()
    for hops in range(5):
        receive(1, hops)
    if middle is None:
        from_sibling(0)
    from_sibling(1)
    for copy in sent:
        copy.wait_send()


Z_STEP = 4
SENDS = 2 * (2 + 2 * (3 + 12 + 16))


def layer_kernel(
    normed_ref, block_ref, cos_ref, sin_ref, start_ref, kv_ref, mix_ref,
    weights, landing, both, landing_kv, queries, mapped,
    send_sem, recv_sem, relay_sem, send_kv, recv_kv, relay_kv,
):
    lines, width = block_ref.shape
    part = width // 2
    rows = kv_ref.shape[1]
    dim = PER_ATTN_DIM
    me = lax.axis_index("dp")
    heads = part // dim

    greet()

    def slot(origin, half):
        return weights.at[half, pl.ds(pl.multiple_of(origin * lines, lines), lines), :]

    own = pl.ds(pl.multiple_of(me * lines, lines), lines)
    for half in range(2):
        weights[half, own, :] = block_ref[:, half * part : (half + 1) * part]

    reach = normed_ref.shape[1] // 2

    def product(half, plane):
        place = pl.ds(pl.multiple_of(plane * reach, reach), reach)
        return jnp.dot(
            normed_ref[:, place], weights[half, place, :], preferred_element_type=jnp.float32
        )

    plane = me // (2 * RING * RING)

    def near():
        for half in range(2):
            mapped[half] = product(half, plane)

    spread(
        lambda half: block_ref.at[:, pl.ds(half * part, part)],
        slot, landing, send_sem, recv_sem, relay_sem, middle=near,
    )

    def kv_slot(origin, half):
        return both.at[half, pl.ds(pl.multiple_of(origin * rows, rows), rows), :]

    mine = pl.ds(pl.multiple_of(me * rows, rows), rows)

    def finish(half):
        result = mapped[half] + product(half, 1 - plane)
        for j in range(heads):
            head = half * heads + j
            vec = result[:, j * dim : (j + 1) * dim]
            if head <= QUARTET_SHARE:
                vec = vec * cos_ref[...] + pltpu.roll(vec, dim // 2, 1) * sin_ref[...]
            vec = vec.astype(jnp.bfloat16)
            if head < QUARTET_SHARE:
                queries[head * rows : (head + 1) * rows, :] = vec
            else:
                kv_ref[head - QUARTET_SHARE] = vec
                both[head - QUARTET_SHARE, mine, :] = vec

    finish(1)
    spread(
        lambda half: kv_ref.at[half],
        kv_slot, landing_kv, send_kv, recv_kv, relay_kv, started=lambda: finish(0),
    )

    step = 512
    inv_root = 1.0 / math.sqrt(dim)
    total_rows = QUARTET_SHARE * rows
    q = queries[...]
    q_start = start_ref[...]
    q_index = me * rows + lax.broadcasted_iota(jnp.int32, (total_rows, 1), 0) % rows
    back = MAXLEN // rows
    low = (jnp.maximum(me - back, 0) * rows) // step
    high = ((me + 1) * rows + step - 1) // step

    def one_step(turn, state):
        top, total, accum = state
        begin = pl.multiple_of(turn * step, step)
        keys = both[0, pl.ds(begin, step), :]
        values = both[1, pl.ds(begin, step), :]
        key_index = begin + lax.broadcasted_iota(jnp.int32, (1, step), 1)
        allowed = (key_index <= q_index) & (key_index >= q_start)
        scores = (
            lax.dot_general(
                q, keys, (((1,), (1,)), ((), ())), preferred_element_type=jnp.float32
            )
            * inv_root
        )
        scores = jnp.where(allowed, scores, masked_score)
        new_top = jnp.maximum(top, jnp.max(scores, axis=1, keepdims=True))
        weight = jnp.where(allowed, jnp.exp(scores - new_top), 0.0)
        fade = jnp.exp(top - new_top)
        total = total * fade + jnp.sum(weight, axis=1, keepdims=True)
        accum = accum * fade + jnp.dot(
            weight.astype(jnp.bfloat16), values, preferred_element_type=jnp.float32
        )
        return new_top, total, accum

    initial = (
        jnp.full((total_rows, 1), masked_score, jnp.float32),
        jnp.zeros((total_rows, 1), jnp.float32),
        jnp.zeros((total_rows, dim), jnp.float32),
    )
    top, total, accum = lax.fori_loop(low, high, one_step, initial)
    mix = (accum / total).astype(jnp.bfloat16)
    for j in range(QUARTET_SHARE):
        mix_ref[:, j * dim : (j + 1) * dim] = mix[j * rows : (j + 1) * rows]


def per_device(
    hidden, norm_gain, learner_probe_proj, learner_lookup_proj, learner_content_proj, lengths
):
    tok_rows = hidden.shape[0]
    learner_lines = learner_probe_proj.shape[0]
    group_width = (QUARTET_SHARE + 2) * PER_ATTN_DIM
    combined_slab = jnp.concatenate(
        [
            learner_probe_proj.reshape(learner_lines, SHARED_KV_NUM, QUARTET_SHARE * PER_ATTN_DIM),
            learner_lookup_proj.reshape(learner_lines, SHARED_KV_NUM, PER_ATTN_DIM),
            learner_content_proj.reshape(learner_lines, SHARED_KV_NUM, PER_ATTN_DIM),
        ],
        axis=2,
    )
    combined_slab = combined_slab.reshape(learner_lines, SHARED_KV_NUM * group_width).astype(
        jnp.bfloat16
    )
    serving_combined = lax.all_to_all(
        combined_slab, "tensor", split_axis=1, concat_axis=0, tiled=True
    )
    widened = hidden.astype(jnp.float32)
    scale = lax.rsqrt(jnp.mean(widened * widened, axis=1, keepdims=True) + norm_eps)
    normed = (widened * scale * norm_gain.astype(jnp.float32)[None, :]).astype(jnp.bfloat16)

    my_index = lax.axis_index("dp") * tok_rows + jnp.arange(tok_rows, dtype=jnp.int32)
    my_start = document_start(lengths, my_index)
    half_dim = PER_ATTN_DIM // 2
    inverse = rope_theta ** (-2.0 * jnp.arange(half_dim, dtype=jnp.float32) / PER_ATTN_DIM)
    angles = (my_index - my_start).astype(jnp.float32)[:, None] * inverse[None, :]
    cosine = jnp.cos(angles)
    sine = jnp.sin(angles)
    cosine = jnp.concatenate([cosine, cosine], axis=1)
    sine = jnp.concatenate([-sine, sine], axis=1)

    rows = serving_combined.shape[0]
    devices = 4 * RING * RING
    part = group_width // 2
    starts = jnp.tile(my_start, QUARTET_SHARE)[:, None]
    vmem = pl.BlockSpec(memory_space=pltpu.VMEM)
    semaphores = [
        pltpu.SemaphoreType.DMA((SENDS,)),
        pltpu.SemaphoreType.DMA((devices, 2)),
        pltpu.SemaphoreType.DMA((2,)),
    ]
    keys_values, attention_mix = pl.pallas_call(
        layer_kernel,
        out_shape=(
            jax.ShapeDtypeStruct((2, tok_rows, PER_ATTN_DIM), jnp.bfloat16),
            jax.ShapeDtypeStruct((tok_rows, QUARTET_SHARE * PER_ATTN_DIM), jnp.bfloat16),
        ),
        in_specs=[vmem] * 5,
        out_specs=(vmem, vmem),
        scratch_shapes=[
            pltpu.VMEM((2, rows * devices, part), jnp.bfloat16),
            pltpu.VMEM((2, rows, part), jnp.bfloat16),
            pltpu.VMEM((2, tok_rows * devices, PER_ATTN_DIM), jnp.bfloat16),
            pltpu.VMEM((2, tok_rows, PER_ATTN_DIM), jnp.bfloat16),
            pltpu.VMEM((QUARTET_SHARE * tok_rows, PER_ATTN_DIM), jnp.bfloat16),
            pltpu.VMEM((2, tok_rows, part), jnp.float32),
        ]
        + semaphores
        + semaphores,
        compiler_params=pltpu.CompilerParams(
            collective_id=0, has_side_effects=True, vmem_limit_bytes=48 * 2**20
        ),
        name="layer",
    )(normed, serving_combined, cosine, sine, starts)
    return (serving_combined, keys_values[0], keys_values[1], attention_mix)


def solution(mesh):
    in_specs = (
        P("dp", None),
        P(),
        P(("dp", "tensor"), None),
        P(("dp", "tensor"), None),
        P(("dp", "tensor"), None),
        P(),
    )
    out_specs = (P("dp", "tensor"), P("dp", "tensor"), P("dp", "tensor"), P("dp", "tensor"))
    return jax.shard_map(
        per_device, mesh=mesh, in_specs=in_specs, out_specs=out_specs, check_vma=False
    )
```

time: 139 us -> 131 us (0.942)
  Pallas kernels: 108 us -> 101 us
  other arithmetic: 5.15 us -> 6.65 us
    pallas_call x2 -> x1, Pallas kernels: 108 us -> 101 us  [per_device(): pl.pallas_call(layer_kernel, out_shape=(jax.ShapeDtypeStruct((2, tok_rows...]
    convert_element_type x1, other arithmetic: 0.51 us -> 2.01 us  [per_device(): (widened * scale * norm_gain.astype(jnp.float32)[None, :]).astype(jnp.bfl...]
  transfers between devices with their start and end apart: 1 -> 1, of which waited for: 1 -> 1; matrix products, arithmetic and copies ran while one was open for 1% -> 3% of each run, Pallas kernels for 0% -> 0%
where the time goes in v2:
time: 131 us; the launch traced here: 130 us
  Pallas kernels  101 us (77%)
  starting transfers between devices  12.2 us (9%)
  waiting for transfers between devices  7.74 us (6%)
  other arithmetic  6.65 us (5%)
  local copies, waits for them, and re-layouts  1.65 us (1%)
    pallas_call x1, Pallas kernels, per_device(): pl.pallas_call(layer_kernel, out_shape=(jax.ShapeDtypeStruct((2, tok_rows...  101 us
    all_to_all x1, starting transfers between devices, per_device(): lax.all_to_all(combined_slab, 'tensor', split_axis=1, concat_axis=0, tile...  12.2 us
    all_to_all x1, waiting for transfers between devices, per_device(): lax.all_to_all(combined_slab, 'tensor', split_axis=1, concat_axis=0, tile...  7.74 us
    another operation x4, other arithmetic  2.97 us
  transfers between devices with their start and end apart: 1, of which 1 were waited for; matrix products, arithmetic and copies ran while one was open for 3% of the time, Pallas kernels for 0%

profile of v2, /device:TPU:25, one launch (start us, length us, event | category | flops | bytes accessed | tf_op | source)
XLA Modules:
  0.0 130.3 jit_solution(9788359665665992917)
XLA Ops:
  0.6 0.0 copy-start.3
  0.6 0.0 copy-start.1
  0.7 1.0 convert.13
  1.7 0.8 convert.14
  2.6 0.0 copy-start.2
  2.6 1.0 convert.12
  3.7 0.7 pad_maximum_fusion
  4.3 12.2 %all-to-all-start = ((bf16[14,8,768]{2,0,1:T(8,128)(2,1)}), bf16[14,8,768]{2,0,1:T(8,128)(2,1)S(1)}, u32[]{:S(2)}, u32[]{:S(2)}) async-start(bf16[14,8,768]{2,0,1:T(8,128)(2,1)} %pad_maximum_fusion), calls=%async_computation | async-start | bytes 393216 | tf_op jit(solution)/shard_map/all_to_all | solution.py:289
  16.6 0.0 copy-done.3
  16.6 0.2 reduce-window.8
  16.8 0.0 copy-done.1
  16.8 0.4 fusion
  17.2 0.0 copy-done.2
  17.3 2.0 %fusion.2.normed_ref = bf16[128,7168]{1,0:T(8,128)(2,1)S(1)} fusion(bf16[128,7168]{1,0:T(8,128)(2,1)} %param.6, f32[7168]{0:T(1024)S(1)} %convert_element_type.19, f32[128]{0:T(128)S(1)} %add_rsqrt_fusion), kind=kLoop, calls=%fused_computation.4 | loop fusion | flops 3670016 | bytes 3699200 | tf_op jit(solution)/shard_map/convert_element_type | solution.py:294
  19.3 0.1 select_reduce_fusion
  19.4 0.2 copy.20.start_ref
  19.6 0.3 fusion.3
  19.9 0.1 pad_maximum_fusion.1
  20.0 7.7 %all-to-all-done = bf16[14,8,768]{2,0,1:T(8,128)(2,1)S(1)} async-done(((bf16[14,8,768]{2,0,1:T(8,128)(2,1)}), bf16[14,8,768]{2,0,1:T(8,128)(2,1)S(1)}, u32[]{:S(2)}, u32[]{:S(2)}) %all-to-all-start) | async-done | bytes 172064 | tf_op jit(solution)/shard_map/all_to_all | solution.py:289
  27.7 0.1 all_to_all.14.block_ref
  27.8 0.0 copy-start
  27.8 101.2 %layer.1 = (bf16[2,128,128]{2,1,0:T(8,128)(2,1)S(1)}, bf16[128,512]{1,0:T(8,128)(2,1)S(1)}) custom-call(bf16[128,7168]{1,0:T(8,128)(2,1)S(1)} %fusion.2.normed_ref, bf16[112,768]{1,0:T(8,128)(2,1)S(1)} %all_to_all.14.block_ref, f32[128,128]{1,0:T(8,128)S(1)} %get-tuple-element.13.cos_ref, f32[128,128]{1,0:T(8,128)S(1)} %get-tuple-element.14.sin_ref, ...), custom_call_target="tpu_custom_call" | custom-call | tf_op jit(solution)/shard_map/layer/pallas_call | solution.py:316
  129.0 0.6 slice_bitcast_fusion
  129.6 0.7 copy.25
  130.3 0.0 copy-done
  (16 shorter events, 0.2 us)
Async XLA Ops:
  0.6 16.0 %copy-start.3 = (s32[4]{0:T(128)S(1)}, s32[4]{0:T(128)}, u32[]{:S(2)}) copy-start(s32[4]{0:T(128)} %param.11) | copy-start | bytes 52
  0.6 16.1 %copy-start.1 = (bf16[128,7168]{1,0:T(8,128)(2,1)S(1)}, bf16[128,7168]{1,0:T(8,128)(2,1)}, u32[]{:S(2)}) copy-start(bf16[128,7168]{1,0:T(8,128)(2,1)} %param.6) | copy-start | bytes 5505028
  2.6 14.7 %copy-start.2 = (bf16[7168]{0:T(1024)(128)(2,1)S(1)}, bf16[7168]{0:T(1024)(128)(2,1)}, u32[]{:S(2)}) copy-start(bf16[7168]{0:T(1024)(128)(2,1)} %param.7) | copy-start | bytes 43012
  4.3 23.4 %all-to-all-start = ((bf16[14,8,768]{2,0,1:T(8,128)(2,1)}), bf16[14,8,768]{2,0,1:T(8,128)(2,1)S(1)}, u32[]{:S(2)}, u32[]{:S(2)}) async-start(bf16[14,8,768]{2,0,1:T(8,128)(2,1)} %pad_maximum_fusion), calls=%async_computation | async-start | bytes 393216 | tf_op jit(solution)/shard_map/all_to_all | solution.py:289
  27.8 102.5 %copy-start = (bf16[112,768]{1,0:T(8,128)(2,1)}, bf16[112,768]{1,0:T(8,128)(2,1)S(1)}, u32[]{:S(2)}) copy-start(bf16[112,768]{1,0:T(8,128)(2,1)S(1)} %all_to_all.14.block_ref) | copy-start | bytes 516100

commit v3 on v2

--- a/solution.py
+++ b/solution.py
@@ -62,7 +62,7 @@
     pl.semaphore_wait(barrier, len(partners))
 
 
-def spread(source, slot, relay, send_sem, recv_sem, relay_sem, started=None, middle=None):
+def spread(source, slot, relay, send_sem, recv_sem, relay_sem, share=True, middle=None):
     me = lax.axis_index("dp")
     core = me % 2
     tensor = lax.axis_index("tensor")
@@ -111,7 +111,8 @@
             give(0, 1)
         if second == 1 and not upward:
             give(0, -1)
-        push(src, slot(origin, half), (sibling, tensor), recv_sem.at[origin, half])
+        if share:
+            push(src, slot(origin, half), (sibling, tensor), recv_sem.at[origin, half])
 
     offsets = [(f, s) for f in (0, -1, 1, 2) for s in (0, -1, 1, 2)]
     offsets.sort(key=lambda pair: abs(pair[0]) + abs(pair[1]))
@@ -134,8 +135,6 @@
         push(source(half), relay.at[half], z_chip(Z_STEP - 2 * Z_STEP * half), relay_sem.at[half])
     for half in range(2):
         forward(source(half), half, 0, 0, 0)
-    if started is not None:
-        started()
     receive(0, 1)
     for half in range(2):
         shift = Z_STEP - 2 * Z_STEP * half
@@ -145,90 +144,118 @@
     for hops in range(2, 5):
         receive(0, hops)
     if middle is not None:
-        from_sibling(0)
         middle()
     for hops in range(5):
         receive(1, hops)
-    if middle is None:
+    if share:
         from_sibling(0)
-    from_sibling(1)
+        from_sibling(1)
     for copy in sent:
         copy.wait_send()
 
 
 Z_STEP = 4
-SENDS = 2 * (2 + 2 * (3 + 12 + 16))
+SENDS = 2 * (2 + 2 * (3 + 12))
+SHARED_SENDS = SENDS + 2 * 2 * 16
 
 
 def layer_kernel(
     normed_ref, block_ref, cos_ref, sin_ref, start_ref, kv_ref, mix_ref,
-    weights, landing, both, landing_kv, queries, mapped,
-    send_sem, recv_sem, relay_sem, send_kv, recv_kv, relay_kv,
+    weights, landing, both, landing_kv, tokens, mapped, made, parts,
+    send_sem, recv_sem, relay_sem, send_kv, recv_kv, relay_kv, pair_send, pair_recv, local_sem,
 ):
     lines, width = block_ref.shape
     part = width // 2
     rows = kv_ref.shape[1]
     dim = PER_ATTN_DIM
     me = lax.axis_index("dp")
+    core = me % 2
     heads = part // dim
 
     greet()
 
+    def pair(src, dst, number):
+        copy = pltpu.make_async_remote_copy(
+            src_ref=src,
+            dst_ref=dst,
+            send_sem=pair_send.at[number],
+            recv_sem=pair_recv.at[number],
+            device_id=(neighbour_index(0, 0, 0, True), lax.axis_index("tensor")),
+            device_id_type=pl.DeviceIdType.MESH,
+        )
+        copy.start()
+        return copy
+
     def slot(origin, half):
-        return weights.at[half, pl.ds(pl.multiple_of(origin * lines, lines), lines), :]
-
-    own = pl.ds(pl.multiple_of(me * lines, lines), lines)
-    for half in range(2):
-        weights[half, own, :] = block_ref[:, half * part : (half + 1) * part]
+        row = (origin // 2 * 2 + half) * lines
+        return weights.at[pl.ds(pl.multiple_of(row, lines), lines), :]
+
+    own = weights.at[pl.ds(pl.multiple_of(me * lines, lines), lines), :]
+    block_swap = pair(
+        block_ref.at[:, pl.ds(pl.multiple_of((1 - core) * part, part), part)], own, 0
+    )
+    keep = pltpu.make_async_copy(
+        block_ref.at[:, pl.ds(pl.multiple_of(core * part, part), part)], own, local_sem.at[0]
+    )
+    keep.start()
+    seat = tokens.at[pl.ds(pl.multiple_of(core * rows, rows), rows), :]
+    token_swap = pair(normed_ref, seat, 1)
+    keep_tokens = pltpu.make_async_copy(normed_ref, seat, local_sem.at[1])
+    keep_tokens.start()
+    keep.wait()
+    block_swap.wait_recv()
 
     reach = normed_ref.shape[1] // 2
-
-    def product(half, plane):
-        place = pl.ds(pl.multiple_of(plane * reach, reach), reach)
+    plane = me // (2 * RING * RING)
+
+    def product(which):
+        place = pl.ds(pl.multiple_of(which * reach, reach), reach)
         return jnp.dot(
-            normed_ref[:, place], weights[half, place, :], preferred_element_type=jnp.float32
-        )
-
-    plane = me // (2 * RING * RING)
+            tokens[:, place], weights[place, :], preferred_element_type=jnp.float32
+        )
 
     def near():
-        for half in range(2):
-            mapped[half] = product(half, plane)
+        keep_tokens.wait()
+        token_swap.wait_recv()
+        mapped[...] = product(plane)
 
     spread(
-        lambda half: block_ref.at[:, pl.ds(half * part, part)],
-        slot, landing, send_sem, recv_sem, relay_sem, middle=near,
-    )
+        lambda half: slot(me, half),
+        slot, landing, send_sem, recv_sem, relay_sem, share=False, middle=near,
+    )
+    block_swap.wait_send()
+    token_swap.wait_send()
+
+    result = mapped[...] + product(1 - plane)
+    for j in range(heads):
+        vec = result[:, j * dim : (j + 1) * dim]
+        spun = vec * cos_ref[...] + pltpu.roll(vec, dim // 2, 1) * sin_ref[...]
+        if j == heads - 1:
+            spun = jnp.where(core == 0, spun, vec)
+        made[j] = spun.astype(jnp.bfloat16)
+    theirs = pl.ds(pl.multiple_of((1 - core) * rows, rows), rows)
+    ours = pl.ds(pl.multiple_of(core * rows, rows), rows)
+    head_swap = pair(made.at[:, theirs, :], parts.at[pl.ds(core * heads, heads)], 2)
+    for j in range(heads):
+        parts[core * heads + j] = made[j, ours, :]
+    head_swap.wait()
 
     def kv_slot(origin, half):
         return both.at[half, pl.ds(pl.multiple_of(origin * rows, rows), rows), :]
 
     mine = pl.ds(pl.multiple_of(me * rows, rows), rows)
-
-    def finish(half):
-        result = mapped[half] + product(half, 1 - plane)
-        for j in range(heads):
-            head = half * heads + j
-            vec = result[:, j * dim : (j + 1) * dim]
-            if head <= QUARTET_SHARE:
-                vec = vec * cos_ref[...] + pltpu.roll(vec, dim // 2, 1) * sin_ref[...]
-            vec = vec.astype(jnp.bfloat16)
-            if head < QUARTET_SHARE:
-                queries[head * rows : (head + 1) * rows, :] = vec
-            else:
-                kv_ref[head - QUARTET_SHARE] = vec
-                both[head - QUARTET_SHARE, mine, :] = vec
-
-    finish(1)
+    for half in range(2):
+        kv_ref[half] = parts[QUARTET_SHARE + half]
+        both[half, mine, :] = parts[QUARTET_SHARE + half]
     spread(
-        lambda half: kv_ref.at[half],
-        kv_slot, landing_kv, send_kv, recv_kv, relay_kv, started=lambda: finish(0),
+        lambda half: parts.at[QUARTET_SHARE + half],
+        kv_slot, landing_kv, send_kv, recv_kv, relay_kv,
     )
 
     step = 512
     inv_root = 1.0 / math.sqrt(dim)
     total_rows = QUARTET_SHARE * rows
-    q = queries[...]
+    q = parts[:QUARTET_SHARE].reshape(total_rows, dim)
     q_start = start_ref[...]
     q_index = me * rows + lax.broadcasted_iota(jnp.int32, (total_rows, 1), 0) % rows
     back = MAXLEN // rows
@@ -295,9 +322,13 @@
 
     my_index = lax.axis_index("dp") * tok_rows + jnp.arange(tok_rows, dtype=jnp.int32)
     my_start = document_start(lengths, my_index)
+    pair_index = (lax.axis_index("dp") // 2) * 2 * tok_rows + jnp.arange(
+        2 * tok_rows, dtype=jnp.int32
+    )
+    pair_start = document_start(lengths, pair_index)
     half_dim = PER_ATTN_DIM // 2
     inverse = rope_theta ** (-2.0 * jnp.arange(half_dim, dtype=jnp.float32) / PER_ATTN_DIM)
-    angles = (my_index - my_start).astype(jnp.float32)[:, None] * inverse[None, :]
+    angles = (pair_index - pair_start).astype(jnp.float32)[:, None] * inverse[None, :]
     cosine = jnp.cos(angles)
     sine = jnp.sin(angles)
     cosine = jnp.concatenate([cosine, cosine], axis=1)
@@ -308,9 +339,16 @@
     part = group_width // 2
     starts = jnp.tile(my_start, QUARTET_SHARE)[:, None]
     vmem = pl.BlockSpec(memory_space=pltpu.VMEM)
-    semaphores = [
-        pltpu.SemaphoreType.DMA((SENDS,)),
-        pltpu.SemaphoreType.DMA((devices, 2)),
+    semaphores = []
+    for sends in (SENDS, SHARED_SENDS):
+        semaphores += [
+            pltpu.SemaphoreType.DMA((sends,)),
+            pltpu.SemaphoreType.DMA((devices, 2)),
+            pltpu.SemaphoreType.DMA((2,)),
+        ]
+    semaphores += [
+        pltpu.SemaphoreType.DMA((3,)),
+        pltpu.SemaphoreType.DMA((3,)),
         pltpu.SemaphoreType.DMA((2,)),
     ]
     keys_values, attention_mix = pl.pallas_call(
@@ -322,14 +360,15 @@
         in_specs=[vmem] * 5,
         out_specs=(vmem, vmem),
         scratch_shapes=[
-            pltpu.VMEM((2, rows * devices, part), jnp.bfloat16),
+            pltpu.VMEM((rows * devices, part), jnp.bfloat16),
             pltpu.VMEM((2, rows, part), jnp.bfloat16),
             pltpu.VMEM((2, tok_rows * devices, PER_ATTN_DIM), jnp.bfloat16),
             pltpu.VMEM((2, tok_rows, PER_ATTN_DIM), jnp.bfloat16),
-            pltpu.VMEM((QUARTET_SHARE * tok_rows, PER_ATTN_DIM), jnp.bfloat16),
-            pltpu.VMEM((2, tok_rows, part), jnp.float32),
+            pltpu.VMEM((2 * tok_rows, hidden.shape[1]), jnp.bfloat16),
+            pltpu.VMEM((2 * tok_rows, part), jnp.float32),
+            pltpu.VMEM((3, 2 * tok_rows, PER_ATTN_DIM), jnp.bfloat16),
+            pltpu.VMEM((6, tok_rows, PER_ATTN_DIM), jnp.bfloat16),
         ]
-        + semaphores
         + semaphores,
         compiler_params=pltpu.CompilerParams(
             collective_id=0, has_side_effects=True, vmem_limit_bytes=48 * 2**20

time: 131 us -> 131 us (level)
  no operation moved by 1% of the time
where the time goes in v3:
time: 131 us
  Pallas kernels  102 us (78%)
  starting transfers between devices  12.2 us (9%)
  waiting for transfers between devices  7.38 us (6%)
  other arithmetic  7 us (5%)
  local copies, waits for them, and re-layouts  1.65 us (1%)
    pallas_call x1, Pallas kernels, per_device(): pl.pallas_call(layer_kernel, out_shape=(jax.ShapeDtypeStruct((2, tok_rows...  102 us
    all_to_all x1, starting transfers between devices, per_device(): lax.all_to_all(combined_slab, 'tensor', split_axis=1, concat_axis=0, tile...  12.2 us
    all_to_all x1, waiting for transfers between devices, per_device(): lax.all_to_all(combined_slab, 'tensor', split_axis=1, concat_axis=0, tile...  7.38 us
    another operation x4, other arithmetic  2.97 us
  transfers between devices with their start and end apart: 1, of which 1 were waited for; matrix products, arithmetic and copies ran while one was open for 3% of the time, Pallas kernels for 0%

profile of v3, /device:TPU:25, one launch (start us, length us, event | category | flops | bytes accessed | tf_op | source)
XLA Modules:
  0.0 131.0 jit_solution(17397948215138383175)
XLA Ops:
  0.6 0.0 copy-start.3
  0.6 0.0 copy-start.1
  0.7 1.0 convert.13
  1.7 0.8 convert.14
  2.6 0.0 copy-start.2
  2.6 1.0 convert.12
  3.7 0.7 pad_maximum_fusion
  4.3 12.2 %all-to-all-start = ((bf16[14,8,768]{2,0,1:T(8,128)(2,1)}), bf16[14,8,768]{2,0,1:T(8,128)(2,1)S(1)}, u32[]{:S(2)}, u32[]{:S(2)}) async-start(bf16[14,8,768]{2,0,1:T(8,128)(2,1)} %pad_maximum_fusion), calls=%async_computation | async-start | bytes 393216 | tf_op jit(solution)/shard_map/all_to_all | solution.py:316
  16.6 0.0 copy-done.3
  16.6 0.2 reduce-window.8
  16.8 0.0 copy-done.1
  16.8 0.4 fusion
  17.3 0.1 select_reduce_fusion.1
  17.4 0.1 select_reduce_fusion
  17.4 0.0 copy-done.2
  17.5 2.0 %fusion.2.normed_ref = bf16[128,7168]{1,0:T(8,128)(2,1)S(1)} fusion(bf16[128,7168]{1,0:T(8,128)(2,1)} %param.6, f32[7168]{0:T(1024)S(1)} %convert_element_type.19, f32[128]{0:T(128)S(1)} %add_rsqrt_fusion), kind=kLoop, calls=%fused_computation.4 | loop fusion | flops 3670016 | bytes 3699200 | tf_op jit(solution)/shard_map/convert_element_type | solution.py:321
  19.5 0.1 copy.20.start_ref
  19.7 0.5 fusion.3
  20.2 0.1 pad_maximum_fusion.1
  20.4 7.4 %all-to-all-done = bf16[14,8,768]{2,0,1:T(8,128)(2,1)S(1)} async-done(((bf16[14,8,768]{2,0,1:T(8,128)(2,1)}), bf16[14,8,768]{2,0,1:T(8,128)(2,1)S(1)}, u32[]{:S(2)}, u32[]{:S(2)}) %all-to-all-start) | async-done | bytes 172064 | tf_op jit(solution)/shard_map/all_to_all | solution.py:316
  27.7 0.1 all_to_all.14.block_ref
  27.8 0.0 copy-start
  27.8 101.9 %layer.1 = (bf16[2,128,128]{2,1,0:T(8,128)(2,1)S(1)}, bf16[128,512]{1,0:T(8,128)(2,1)S(1)}) custom-call(bf16[128,7168]{1,0:T(8,128)(2,1)S(1)} %fusion.2.normed_ref, bf16[112,768]{1,0:T(8,128)(2,1)S(1)} %all_to_all.14.block_ref, f32[256,128]{1,0:T(8,128)S(1)} %get-tuple-element.13.cos_ref, f32[256,128]{1,0:T(8,128)S(1)} %get-tuple-element.14.sin_ref, ...), custom_call_target="tpu_custom_call" | custom-call | tf_op jit(solution)/shard_map/layer/pallas_call | solution.py:354
  129.7 0.6 slice_bitcast_fusion
  130.3 0.7 copy.25
  131.0 0.0 copy-done
  (17 shorter events, 0.2 us)
Async XLA Ops:
  0.6 16.0 %copy-start.3 = (s32[4]{0:T(128)S(1)}, s32[4]{0:T(128)}, u32[]{:S(2)}) copy-start(s32[4]{0:T(128)} %param.11) | copy-start | bytes 52
  0.6 16.2 %copy-start.1 = (bf16[128,7168]{1,0:T(8,128)(2,1)S(1)}, bf16[128,7168]{1,0:T(8,128)(2,1)}, u32[]{:S(2)}) copy-start(bf16[128,7168]{1,0:T(8,128)(2,1)} %param.6) | copy-start | bytes 5505028
  2.6 14.9 %copy-start.2 = (bf16[7168]{0:T(1024)(128)(2,1)S(1)}, bf16[7168]{0:T(1024)(128)(2,1)}, u32[]{:S(2)}) copy-start(bf16[7168]{0:T(1024)(128)(2,1)} %param.7) | copy-start | bytes 43012
  4.3 23.4 %all-to-all-start = ((bf16[14,8,768]{2,0,1:T(8,128)(2,1)}), bf16[14,8,768]{2,0,1:T(8,128)(2,1)S(1)}, u32[]{:S(2)}, u32[]{:S(2)}) async-start(bf16[14,8,768]{2,0,1:T(8,128)(2,1)} %pad_maximum_fusion), calls=%async_computation | async-start | bytes 393216 | tf_op jit(solution)/shard_map/all_to_all | solution.py:316
  27.8 103.2 %copy-start = (bf16[112,768]{1,0:T(8,128)(2,1)}, bf16[112,768]{1,0:T(8,128)(2,1)S(1)}, u32[]{:S(2)}) copy-start(bf16[112,768]{1,0:T(8,128)(2,1)S(1)} %all_to_all.14.block_ref) | copy-start | bytes 516100

commit v4 on v3

--- a/solution.py
+++ b/solution.py
@@ -62,7 +62,7 @@
     pl.semaphore_wait(barrier, len(partners))
 
 
-def spread(source, slot, relay, send_sem, recv_sem, relay_sem, share=True, middle=None):
+def spread(source, slot, relay, send_sem, recv_sem, relay_sem, share, middle, after=None):
     me = lax.axis_index("dp")
     core = me % 2
     tensor = lax.axis_index("tensor")
@@ -125,9 +125,11 @@
                     landed(slot(origin, half), recv_sem.at[origin, half])
                     forward(slot(origin, half), half, dz, first, second)
 
-    def from_sibling(dz):
+    def from_sibling(dz, lanes=(0, -1, 1, 2)):
         for first, second in offsets:
             for half in range(2):
+                if (second if half == 0 else first) not in lanes:
+                    continue
                 origin = along(half, dz, first, second) + 1 - 2 * core
                 landed(slot(origin, half), recv_sem.at[origin, half])
 
@@ -143,13 +145,11 @@
         push(relay.at[half], slot(origin, half), z_chip(shift), recv_sem.at[origin, half])
     for hops in range(2, 5):
         receive(0, hops)
-    if middle is not None:
-        middle()
+    middle(from_sibling)
     for hops in range(5):
         receive(1, hops)
-    if share:
-        from_sibling(0)
-        from_sibling(1)
+        if after is not None:
+            after(hops, from_sibling)
     for copy in sent:
         copy.wait_send()
 
@@ -214,14 +214,14 @@
             tokens[:, place], weights[place, :], preferred_element_type=jnp.float32
         )
 
-    def near():
+    def near(_):
         keep_tokens.wait()
         token_swap.wait_recv()
         mapped[...] = product(plane)
 
     spread(
         lambda half: slot(me, half),
-        slot, landing, send_sem, recv_sem, relay_sem, share=False, middle=near,
+        slot, landing, send_sem, recv_sem, relay_sem, False, near,
     )
     block_swap.wait_send()
     token_swap.wait_send()
@@ -247,11 +247,6 @@
     for half in range(2):
         kv_ref[half] = parts[QUARTET_SHARE + half]
         both[half, mine, :] = parts[QUARTET_SHARE + half]
-    spread(
-        lambda half: parts.at[QUARTET_SHARE + half],
-        kv_slot, landing_kv, send_kv, recv_kv, relay_kv,
-    )
-
     step = 512
     inv_root = 1.0 / math.sqrt(dim)
     total_rows = QUARTET_SHARE * rows
@@ -277,7 +272,7 @@
         )
         scores = jnp.where(allowed, scores, masked_score)
         new_top = jnp.maximum(top, jnp.max(scores, axis=1, keepdims=True))
-        weight = jnp.where(allowed, jnp.exp(scores - new_top), 0.0)
+        weight = jnp.exp(scores - new_top)
         fade = jnp.exp(top - new_top)
         total = total * fade + jnp.sum(weight, axis=1, keepdims=True)
         accum = accum * fade + jnp.dot(
@@ -290,7 +285,46 @@
         jnp.zeros((total_rows, 1), jnp.float32),
         jnp.zeros((total_rows, dim), jnp.float32),
     )
-    top, total, accum = lax.fori_loop(low, high, one_step, initial)
+    state = [initial]
+
+    def run(begin, end):
+        count = jnp.maximum(end - begin, 0)
+        state[0] = lax.fori_loop(
+            0, count, lambda turn, held: one_step(end - 1 - turn, held), state[0]
+        )
+
+    half_steps = MAXLEN // step
+    own_low = jnp.maximum(low, half_steps * plane)
+    marks = [high] + [jnp.maximum(own_low, high - k) for k in (4, 6, half_steps)]
+    y = (me // (2 * RING)) % RING
+    row_steps = half_steps // RING
+
+    def far_row(dy):
+        first_step = (y + dy + RING) % RING * row_steps
+        run(jnp.maximum(first_step, low), jnp.minimum(first_step + row_steps, half_steps * plane))
+
+    def near_keys(from_sibling):
+        from_sibling(0)
+        run(marks[1], marks[0])
+
+    def far_keys(hops, from_sibling):
+        if hops in (1, 2):
+            run(marks[hops + 1], marks[hops])
+        if hops == 3:
+            from_sibling(1, (0,))
+            far_row(0)
+        if hops == 4:
+            from_sibling(1, (-1, 1))
+            far_row(-1)
+            far_row(1)
+            from_sibling(1, (2,))
+            far_row(2)
+
+    spread(
+        lambda half: parts.at[QUARTET_SHARE + half],
+        kv_slot, landing_kv, send_kv, recv_kv, relay_kv, True, near_keys, far_keys,
+    )
+    top, total, accum = state[0]
     mix = (accum / total).astype(jnp.bfloat16)
     for j in range(QUARTET_SHARE):
         mix_ref[:, j * dim : (j + 1) * dim] = mix[j * rows : (j + 1) * rows]

time: 131 us -> 129 us (0.985)
  Pallas kernels: 102 us -> 99 us
    pallas_call x1, Pallas kernels: 102 us -> 99 us  [per_device(): pl.pallas_call(layer_kernel, out_shape=(jax.ShapeDtypeStruct((2, tok_rows...]
where the time goes in v4:
time: 129 us; the launch traced here: 128 us
  Pallas kernels  99 us (77%)
  starting transfers between devices  12.2 us (9%)
  waiting for transfers between devices  7.38 us (6%)
  other arithmetic  7 us (5%)
  local copies, waits for them, and re-layouts  1.65 us (1%)
    pallas_call x1, Pallas kernels, per_device(): pl.pallas_call(layer_kernel, out_shape=(jax.ShapeDtypeStruct((2, tok_rows...  99 us
    all_to_all x1, starting transfers between devices, per_device(): lax.all_to_all(combined_slab, 'tensor', split_axis=1, concat_axis=0, tile...  12.2 us
    all_to_all x1, waiting for transfers between devices, per_device(): lax.all_to_all(combined_slab, 'tensor', split_axis=1, concat_axis=0, tile...  7.38 us
    another operation x4, other arithmetic  2.97 us
  transfers between devices with their start and end apart: 1, of which 1 were waited for; matrix products, arithmetic and copies ran while one was open for 3% of the time, Pallas kernels for 0%

profile of v4, /device:TPU:25, one launch (start us, length us, event | category | flops | bytes accessed | tf_op | source)
XLA Modules:
  0.0 128.1 jit_solution(120056168226051476)
XLA Ops:
  0.6 0.0 copy-start.3
  0.6 0.0 copy-start.1
  0.7 1.0 convert.13
  1.7 0.8 convert.14
  2.6 0.0 copy-start.2
  2.6 1.0 convert.12
  3.7 0.7 pad_maximum_fusion
  4.3 12.2 %all-to-all-start = ((bf16[14,8,768]{2,0,1:T(8,128)(2,1)}), bf16[14,8,768]{2,0,1:T(8,128)(2,1)S(1)}, u32[]{:S(2)}, u32[]{:S(2)}) async-start(bf16[14,8,768]{2,0,1:T(8,128)(2,1)} %pad_maximum_fusion), calls=%async_computation | async-start | bytes 393216 | tf_op jit(solution)/shard_map/all_to_all | solution.py:350
  16.6 0.0 copy-done.3
  16.6 0.2 reduce-window.8
  16.8 0.0 copy-done.1
  16.8 0.4 fusion
  17.3 0.1 select_reduce_fusion.1
  17.4 0.1 select_reduce_fusion
  17.4 0.0 copy-done.2
  17.5 2.0 %fusion.2.normed_ref = bf16[128,7168]{1,0:T(8,128)(2,1)S(1)} fusion(bf16[128,7168]{1,0:T(8,128)(2,1)} %param.6, f32[7168]{0:T(1024)S(1)} %convert_element_type.19, f32[128]{0:T(128)S(1)} %add_rsqrt_fusion), kind=kLoop, calls=%fused_computation.4 | loop fusion | flops 3670016 | bytes 3699200 | tf_op jit(solution)/shard_map/convert_element_type | solution.py:355
  19.5 0.1 copy.20.start_ref
  19.7 0.5 fusion.3
  20.2 0.1 pad_maximum_fusion.1
  20.4 7.4 %all-to-all-done = bf16[14,8,768]{2,0,1:T(8,128)(2,1)S(1)} async-done(((bf16[14,8,768]{2,0,1:T(8,128)(2,1)}), bf16[14,8,768]{2,0,1:T(8,128)(2,1)S(1)}, u32[]{:S(2)}, u32[]{:S(2)}) %all-to-all-start) | async-done | bytes 172064 | tf_op jit(solution)/shard_map/all_to_all | solution.py:350
  27.7 0.1 all_to_all.14.block_ref
  27.8 0.0 copy-start
  27.8 99.0 %layer.1 = (bf16[2,128,128]{2,1,0:T(8,128)(2,1)S(1)}, bf16[128,512]{1,0:T(8,128)(2,1)S(1)}) custom-call(bf16[128,7168]{1,0:T(8,128)(2,1)S(1)} %fusion.2.normed_ref, bf16[112,768]{1,0:T(8,128)(2,1)S(1)} %all_to_all.14.block_ref, f32[256,128]{1,0:T(8,128)S(1)} %get-tuple-element.13.cos_ref, f32[256,128]{1,0:T(8,128)S(1)} %get-tuple-element.14.sin_ref, ...), custom_call_target="tpu_custom_call" | custom-call | tf_op jit(solution)/shard_map/layer/pallas_call | solution.py:388
  126.8 0.6 slice_bitcast_fusion
  127.4 0.7 copy.25
  128.1 0.0 copy-done
  (17 shorter events, 0.2 us)
Async XLA Ops:
  0.6 16.0 %copy-start.3 = (s32[4]{0:T(128)S(1)}, s32[4]{0:T(128)}, u32[]{:S(2)}) copy-start(s32[4]{0:T(128)} %param.11) | copy-start | bytes 52
  0.6 16.2 %copy-start.1 = (bf16[128,7168]{1,0:T(8,128)(2,1)S(1)}, bf16[128,7168]{1,0:T(8,128)(2,1)}, u32[]{:S(2)}) copy-start(bf16[128,7168]{1,0:T(8,128)(2,1)} %param.6) | copy-start | bytes 5505028
  2.6 14.9 %copy-start.2 = (bf16[7168]{0:T(1024)(128)(2,1)S(1)}, bf16[7168]{0:T(1024)(128)(2,1)}, u32[]{:S(2)}) copy-start(bf16[7168]{0:T(1024)(128)(2,1)} %param.7) | copy-start | bytes 43012
  4.3 23.4 %all-to-all-start = ((bf16[14,8,768]{2,0,1:T(8,128)(2,1)}), bf16[14,8,768]{2,0,1:T(8,128)(2,1)S(1)}, u32[]{:S(2)}, u32[]{:S(2)}) async-start(bf16[14,8,768]{2,0,1:T(8,128)(2,1)} %pad_maximum_fusion), calls=%async_computation | async-start | bytes 393216 | tf_op jit(solution)/shard_map/all_to_all | solution.py:350
  27.8 100.3 %copy-start = (bf16[112,768]{1,0:T(8,128)(2,1)}, bf16[112,768]{1,0:T(8,128)(2,1)S(1)}, u32[]{:S(2)}) copy-start(bf16[112,768]{1,0:T(8,128)(2,1)S(1)} %all_to_all.14.block_ref) | copy-start | bytes 516100

commit v5 on v4

--- a/solution.py
+++ b/solution.py
@@ -295,7 +295,7 @@
 
     half_steps = MAXLEN // step
     own_low = jnp.maximum(low, half_steps * plane)
-    marks = [high] + [jnp.maximum(own_low, high - k) for k in (4, 6, half_steps)]
+    marks = [high] + [jnp.maximum(own_low, high - k) for k in (2, 3, 4, half_steps)]
     y = (me // (2 * RING)) % RING
     row_steps = half_steps // RING
 
@@ -308,7 +308,7 @@
         run(marks[1], marks[0])
 
     def far_keys(hops, from_sibling):
-        if hops in (1, 2):
+        if hops in (1, 2, 3):
             run(marks[hops + 1], marks[hops])
         if hops == 3:
             from_sibling(1, (0,))

time: 129 us -> 128 us (level)
  Pallas kernels: 99 us -> 97.5 us
    pallas_call x1, Pallas kernels: 99 us -> 97.5 us  [per_device(): pl.pallas_call(layer_kernel, out_shape=(jax.ShapeDtypeStruct((2, tok_rows...]
where the time goes in v5:
time: 128 us; the launch traced here: 127 us
  Pallas kernels  97.5 us (76%)
  starting transfers between devices  12.2 us (10%)
  waiting for transfers between devices  7.38 us (6%)
  other arithmetic  7 us (5%)
  local copies, waits for them, and re-layouts  1.65 us (1%)
    pallas_call x1, Pallas kernels, per_device(): pl.pallas_call(layer_kernel, out_shape=(jax.ShapeDtypeStruct((2, tok_rows...  97.5 us
    all_to_all x1, starting transfers between devices, per_device(): lax.all_to_all(combined_slab, 'tensor', split_axis=1, concat_axis=0, tile...  12.2 us
    all_to_all x1, waiting for transfers between devices, per_device(): lax.all_to_all(combined_slab, 'tensor', split_axis=1, concat_axis=0, tile...  7.38 us
    another operation x4, other arithmetic  2.97 us
  transfers between devices with their start and end apart: 1, of which 1 were waited for; matrix products, arithmetic and copies ran while one was open for 3% of the time, Pallas kernels for 0%

profile of v5, /device:TPU:25, one launch (start us, length us, event | category | flops | bytes accessed | tf_op | source)
XLA Modules:
  0.0 126.6 jit_solution(2079739098637231701)
XLA Ops:
  0.6 0.0 copy-start.3
  0.6 0.0 copy-start.1
  0.7 1.0 convert.13
  1.7 0.8 convert.14
  2.6 0.0 copy-start.2
  2.6 1.0 convert.12
  3.7 0.7 pad_maximum_fusion
  4.3 12.2 %all-to-all-start = ((bf16[14,8,768]{2,0,1:T(8,128)(2,1)}), bf16[14,8,768]{2,0,1:T(8,128)(2,1)S(1)}, u32[]{:S(2)}, u32[]{:S(2)}) async-start(bf16[14,8,768]{2,0,1:T(8,128)(2,1)} %pad_maximum_fusion), calls=%async_computation | async-start | bytes 393216 | tf_op jit(solution)/shard_map/all_to_all | solution.py:350
  16.6 0.0 copy-done.3
  16.6 0.2 reduce-window.8
  16.8 0.0 copy-done.1
  16.8 0.4 fusion
  17.3 0.1 select_reduce_fusion.1
  17.4 0.1 select_reduce_fusion
  17.4 0.0 copy-done.2
  17.5 2.0 %fusion.2.normed_ref = bf16[128,7168]{1,0:T(8,128)(2,1)S(1)} fusion(bf16[128,7168]{1,0:T(8,128)(2,1)} %param.6, f32[7168]{0:T(1024)S(1)} %convert_element_type.19, f32[128]{0:T(128)S(1)} %add_rsqrt_fusion), kind=kLoop, calls=%fused_computation.4 | loop fusion | flops 3670016 | bytes 3699200 | tf_op jit(solution)/shard_map/convert_element_type | solution.py:355
  19.5 0.1 copy.20.start_ref
  19.7 0.5 fusion.3
  20.2 0.1 pad_maximum_fusion.1
  20.4 7.4 %all-to-all-done = bf16[14,8,768]{2,0,1:T(8,128)(2,1)S(1)} async-done(((bf16[14,8,768]{2,0,1:T(8,128)(2,1)}), bf16[14,8,768]{2,0,1:T(8,128)(2,1)S(1)}, u32[]{:S(2)}, u32[]{:S(2)}) %all-to-all-start) | async-done | bytes 172064 | tf_op jit(solution)/shard_map/all_to_all | solution.py:350
  27.7 0.1 all_to_all.14.block_ref
  27.8 0.0 copy-start
  27.8 97.5 %layer.1 = (bf16[2,128,128]{2,1,0:T(8,128)(2,1)S(1)}, bf16[128,512]{1,0:T(8,128)(2,1)S(1)}) custom-call(bf16[128,7168]{1,0:T(8,128)(2,1)S(1)} %fusion.2.normed_ref, bf16[112,768]{1,0:T(8,128)(2,1)S(1)} %all_to_all.14.block_ref, f32[256,128]{1,0:T(8,128)S(1)} %get-tuple-element.13.cos_ref, f32[256,128]{1,0:T(8,128)S(1)} %get-tuple-element.14.sin_ref, ...), custom_call_target="tpu_custom_call" | custom-call | tf_op jit(solution)/shard_map/layer/pallas_call | solution.py:388
  125.4 0.6 slice_bitcast_fusion
  126.0 0.7 copy.25
  126.6 0.0 copy-done
  (17 shorter events, 0.2 us)
Async XLA Ops:
  0.6 16.0 %copy-start.3 = (s32[4]{0:T(128)S(1)}, s32[4]{0:T(128)}, u32[]{:S(2)}) copy-start(s32[4]{0:T(128)} %param.11) | copy-start | bytes 52
  0.6 16.2 %copy-start.1 = (bf16[128,7168]{1,0:T(8,128)(2,1)S(1)}, bf16[128,7168]{1,0:T(8,128)(2,1)}, u32[]{:S(2)}) copy-start(bf16[128,7168]{1,0:T(8,128)(2,1)} %param.6) | copy-start | bytes 5505028
  2.6 14.9 %copy-start.2 = (bf16[7168]{0:T(1024)(128)(2,1)S(1)}, bf16[7168]{0:T(1024)(128)(2,1)}, u32[]{:S(2)}) copy-start(bf16[7168]{0:T(1024)(128)(2,1)} %param.7) | copy-start | bytes 43012
  4.3 23.4 %all-to-all-start = ((bf16[14,8,768]{2,0,1:T(8,128)(2,1)}), bf16[14,8,768]{2,0,1:T(8,128)(2,1)S(1)}, u32[]{:S(2)}, u32[]{:S(2)}) async-start(bf16[14,8,768]{2,0,1:T(8,128)(2,1)} %pad_maximum_fusion), calls=%async_computation | async-start | bytes 393216 | tf_op jit(solution)/shard_map/all_to_all | solution.py:350
  27.8 98.9 %copy-start = (bf16[112,768]{1,0:T(8,128)(2,1)}, bf16[112,768]{1,0:T(8,128)(2,1)S(1)}, u32[]{:S(2)}) copy-start(bf16[112,768]{1,0:T(8,128)(2,1)S(1)} %all_to_all.14.block_ref) | copy-start | bytes 516100
